TPU v7x, 32 devices: a whole 2x2x4 slice. The times are simulated.
32 devices in a mesh: snap: 2 (over x), gx: 16 (over z, y, core).
Axes of the slice: x: 2, y: 2, z: 4, core: 2. Of those that a mesh axis runs over, the one named last changes fastest.
Arguments:
- component_shares: float32 [22, 160, 32, 128], P(None, ('snap', 'gx')), parts along dimension 1, may hold values from 0.01 to 1
- thermal_ratio: float32 [160, 32, 128], P(('snap', 'gx')), parts along dimension 0, may hold values from 0.5 to 2.5
- fuel_share: float32 [160, 32, 128], P(('snap', 'gx')), parts along dimension 0, may hold values from 0 to 1
- species_mass_unit: float32 [22], replicated, may hold values from 0.5 to 2
- formation_energy: float32 [22], replicated, may hold values from -4 to 4
- frequency_factor: float32 [206], replicated, may hold values from 0.5 to 2
- arrhenius_barrier: float32 [206], replicated, may hold values from 0.5 to 4
- product_minus_reactant: int32 [206, 22], replicated, may hold values from -1 to 2, as said below
- particle_voxel_position: int32 [32, 16, 64], P(('snap', 'gx')), parts along dimension 0, may hold values from 0 to 20479, as said below
- particle_voxel_offset: float32 [32, 16, 3, 64], P(('snap', 'gx')), parts along dimension 0, may hold values from 0 to 1
- particle_active_total: int32 [32, 16], P(('snap', 'gx')), parts along dimension 0, may hold values from 0 to 64, as said below
Outputs:
- samples: float32 [32, 16, 4, 64], P(('snap', 'gx')), parts along dimension 0
There are 2 independent parts, one for each index of `snap`. A program takes and returns all parts, laid end to end along the dimension named above; an argument that names none is the same for every part. Nothing has to cross between parts.
Inputs may be any that keep to these rules, and one draw needn't show every extreme that they name: `product_minus_reactant`: each row has two reactants of coefficient -1 and two products of coefficient 1 or 2, at four different species. `particle_voxel_position`: every slot, live or not, names a cell of its owner brick, flattened as (plane * 32 + y) * 128 + z with plane below 5. `particle_active_total`: at most 64; in every draw some owner brick receives 64 live tracers from every source device.
All inputs are finite; a program needn't handle non-finite values.
Results may differ from a plain program's by a relative error of at most 0.000068.
Values sent between devices are 32-bit elements; how exact they have to be, the bound alone decides.
A program may use at most 64 MiB of HBM per device.

v0:
```python
import math

import jax
import jax.numpy as jnp
from jax import lax
from jax.sharding import PartitionSpec as P

stencil_coeffs = (0.8, -0.2, 4.0 / 105.0, -1.0 / 280.0)
highest_precision = lax.Precision.HIGHEST


def with_halo(x, sides, width):
    for axis, dim in sides:
        count, length = (lax.axis_size(axis), x.shape[dim])
        up = [(i, (i + 1) % count) for i in range(count)]
        down = [(j, i) for i, j in up]
        last = lax.slice_in_dim(x, length - width, length, axis=dim)
        first = lax.slice_in_dim(x, 0, width, axis=dim)
        before = lax.ppermute(last, axis, up)
        after = lax.ppermute(first, axis, down)
        x = jnp.concatenate([before, x, after], axis=dim)
    return x


def from_behind(x, axis, by):
    count = lax.axis_size(axis)
    return lax.ppermute(x, axis, [(i, (i + by) % count) for i in range(count)])


def heat_block(
    species_block,
    temper,
    kinetic_exponents,
    combined_thermal_output,
    log_rate_prefactor,
    arrhenius_barrier,
    log_molar_weight,
):
    log_conc = jnp.log(species_block) - log_molar_weight[:, None] - jnp.log(temper)[None, :]
    log_rate = jnp.dot(
        kinetic_exponents, log_conc, precision=highest_precision, preferred_element_type=jnp.float32
    )
    log_rate = log_rate + log_rate_prefactor[:, None] - arrhenius_barrier[:, None] / temper[None, :]
    return -jnp.dot(
        combined_thermal_output,
        jnp.exp(log_rate),
        precision=highest_precision,
        preferred_element_type=jnp.float32,
    )


def thermal_output_grid(
    species_part,
    temper_part,
    kinetic_exponents,
    combined_thermal_output,
    log_rate_prefactor,
    arrhenius_barrier,
    log_molar_weight,
):
    species_flat = species_part.reshape(species_part.shape[0], -1)
    temper_flat = temper_part.reshape(-1)
    cells = temper_flat.shape[0]
    block_len = math.gcd(cells, 8192)
    blocks = cells // block_len

    def thermal_one_block(index):
        start = index * block_len
        return heat_block(
            lax.dynamic_slice_in_dim(species_flat, start, block_len, 1),
            lax.dynamic_slice_in_dim(temper_flat, start, block_len, 0),
            kinetic_exponents,
            combined_thermal_output,
            log_rate_prefactor,
            arrhenius_barrier,
            log_molar_weight,
        )

    return lax.map(thermal_one_block, jnp.arange(blocks, dtype=jnp.int32)).reshape(
        temper_part.shape
    )


def cross_gradient(field, axis):
    total = jnp.zeros_like(field)
    for offset in range(1, 5):
        coeff = stencil_coeffs[offset - 1]
        total = total + coeff * (jnp.roll(field, -offset, axis) - jnp.roll(field, offset, axis))
    return total


def mixing_decay_grid(bordered_grid, margin, slice_pile, temper):
    centre = bordered_grid[margin : margin + slice_pile]
    grad_x = jnp.zeros_like(centre)
    for offset in range(1, 5):
        coeff = stencil_coeffs[offset - 1]
        grad_x = grad_x + coeff * (
            bordered_grid[margin + offset : margin + offset + slice_pile]
            - bordered_grid[margin - offset : margin - offset + slice_pile]
        )
    grad_y = cross_gradient(centre, 1)
    grad_z = cross_gradient(centre, 2)
    smoothed_quantity = 0.5 * jnp.power(temper, 0.7)
    return 2.0 * smoothed_quantity * (grad_x * grad_x + grad_y * grad_y + grad_z * grad_z)


def two_hot(count, lower, frac, wraps):
    labels = jnp.arange(count, dtype=jnp.int32)[:, None]
    upper = (lower + 1) % count if wraps else lower + 1
    return (labels == lower[None, :]).astype(jnp.float32) * (1.0 - frac)[None, :] + (
        labels == upper[None, :]
    ).astype(jnp.float32) * frac[None, :]


def interpolate(quantity_pile, cell_index, fracs, box_length_first, box_length_second):
    planes = quantity_pile.shape[1]
    field_rows = quantity_pile.reshape(4 * planes * box_length_first, box_length_second)
    sources, slots = cell_index.shape
    total_slots = sources * slots
    flat_index = cell_index.reshape(total_slots)
    flat_fracs = jnp.transpose(fracs, (1, 0, 2)).reshape(3, total_slots)
    block_len = math.gcd(total_slots, 2048)
    blocks = total_slots // block_len

    def interpolate_one_block(index):
        start = index * block_len
        cells = lax.dynamic_slice_in_dim(flat_index, start, block_len, 0)
        part_fracs = lax.dynamic_slice_in_dim(flat_fracs, start, block_len, 1)
        cell_x = cells // (box_length_first * box_length_second)
        cell_y = cells // box_length_second % box_length_first
        cell_z = cells % box_length_second
        weight_z = two_hot(box_length_second, cell_z, part_fracs[2], True)
        weight_y = two_hot(box_length_first, cell_y, part_fracs[1], True)
        weight_x = two_hot(planes, cell_x, part_fracs[0], False)
        along_z = jnp.dot(
            field_rows, weight_z, precision=highest_precision, preferred_element_type=jnp.float32
        )
        along_z = along_z.reshape(4, planes * box_length_first, block_len)
        weight_xy = (weight_x[:, None, :] * weight_y[None, :, :]).reshape(
            planes * box_length_first, block_len
        )
        return jnp.sum(along_z * weight_xy[None], axis=1)

    values = lax.map(interpolate_one_block, jnp.arange(blocks, dtype=jnp.int32))
    values = jnp.transpose(values, (1, 0, 2)).reshape(4, sources, slots)
    return jnp.transpose(values, (1, 0, 2))


def local(
    component_shares,
    thermal_ratio,
    fuel_share,
    species_mass_unit,
    formation_energy,
    frequency_factor,
    arrhenius_barrier,
    product_minus_reactant,
    particle_voxel_position,
    particle_voxel_offset,
    particle_active_total,
):
    kinetic_exponents = jnp.maximum(-product_minus_reactant, 0).astype(jnp.float32)
    combined_thermal_output = jnp.dot(
        product_minus_reactant.astype(jnp.float32),
        formation_energy,
        precision=highest_precision,
        preferred_element_type=jnp.float32,
    )
    log_rate_prefactor = jnp.log(frequency_factor)
    log_molar_weight = jnp.log(species_mass_unit)
    slice_pile, box_length_first, box_length_second = thermal_ratio.shape
    bordered_grid = with_halo(fuel_share, (("gx", 0),), 5)
    next_temper, next_species = from_behind(
        (thermal_ratio[0:1], component_shares[:, 0:1]), "gx", -1
    )
    temper_ext = jnp.concatenate([thermal_ratio, next_temper], axis=0)
    gradient_squared_mixing = mixing_decay_grid(bordered_grid, 5, slice_pile + 1, temper_ext)
    thermal_output = jnp.concatenate(
        [
            thermal_output_grid(
                component_shares,
                thermal_ratio,
                kinetic_exponents,
                combined_thermal_output,
                log_rate_prefactor,
                arrhenius_barrier,
                log_molar_weight,
            ),
            thermal_output_grid(
                next_species,
                next_temper,
                kinetic_exponents,
                combined_thermal_output,
                log_rate_prefactor,
                arrhenius_barrier,
                log_molar_weight,
            ),
        ],
        axis=0,
    )
    quantity_pile = jnp.stack(
        [temper_ext, bordered_grid[5 : 6 + slice_pile], gradient_squared_mixing, thermal_output]
    )
    outgoing = (
        particle_voxel_position[0].astype(jnp.float32)[:, None, :],
        particle_voxel_offset[0],
    )
    cell_float = lax.all_to_all(outgoing[0], "gx", split_axis=0, concat_axis=0, tiled=True)
    fracs = lax.all_to_all(outgoing[1], "gx", split_axis=0, concat_axis=0, tiled=True)
    sampled = interpolate(
        quantity_pile,
        cell_float[:, 0, :].astype(jnp.int32),
        fracs,
        box_length_first,
        box_length_second,
    )
    returned = lax.all_to_all(sampled, "gx", split_axis=0, concat_axis=0, tiled=True)
    slots = returned.shape[2]
    live_slot = jnp.arange(slots, dtype=jnp.int32)[None, :] < particle_active_total[0][:, None]
    return jnp.where(live_slot[:, None, :], returned, jnp.float32(0.0))[None]


def solution(mesh):
    placed = (
        P(None, ("snap", "gx"), None, None),
        P(("snap", "gx"), None, None),
        P(("snap", "gx"), None, None),
        P(),
        P(),
        P(),
        P(),
        P(),
        P(("snap", "gx"), None, None),
        P(("snap", "gx"), None, None, None),
        P(("snap", "gx"), None),
    )
    return jax.shard_map(
        local,
        mesh=mesh,
        in_specs=placed,
        out_specs=P(("snap", "gx"), None, None, None),
        check_vma=False,
    )
```

profile of v0, /device:TPU:0, one launch (start us, length us, event | category | flops | bytes accessed | tf_op | source)
XLA Modules:
  0.0 93.6 jit_solution(6645243175368144756)
XLA Ops:
  0.5 5.0 %collective-permute-start.1 = (f32[5,32,128]{2,1,0:T(8,128)}, f32[5,32,128]{2,1,0:T(8,128)S(1)}, u32[]{:S(2)}, u32[]{:S(2)}) collective-permute-start(f32[5,32,128]{2,1,0:T(8,128)} %param.15), channel_id=1, source_target_pairs={{1,0},{2,1},{3,2},{4,3},{5,4},{6,5},{7,6},{8,7},{9,8},{10,9},{11,1... | collective-permute-start | bytes 245768 | tf_op jit(solution)/shard_map/ppermute | solution.py:20
  5.5 1.3 %convert_element_type.59 = f32[1,16,64]{2,1,0:T(8,128)} convert(s32[1,16,64]{2,1,0:T(8,128)} %param.21) | non-fusion elementwise | flops 1024 | bytes 8192 | tf_op jit(solution)/shard_map/convert_element_type | solution.py:205
  6.8 3.6 %all-to-all-start = ((f32[16,1,64]{2,1,0:T(1,128)}), f32[16,1,64]{2,1,0:T(1,128)S(1)}, u32[]{:S(2)}, u32[]{:S(2)}) async-start(f32[16,1,64]{2,1,0:T(1,128)} %bitcast.17), calls=%async_computation | async-start | bytes 16384 | tf_op jit(solution)/shard_map/all_to_all | solution.py:208
  11.2 4.3 %collective-permute-start = (f32[1,32,128]{2,1,0:T(8,128)S(1)}, f32[1,32,128]{2,1,0:T(8,128)S(1)}, u32[]{:S(2)}, u32[]{:S(2)}) collective-permute-start(f32[1,32,128]{2,1,0:T(8,128)S(1)} %slice.218), channel_id=1, source_target_pairs={{0,15},{1,0},{2,1},{3,2},{4,3},{5,4},{6,5},{7,6},{8,7},{9,8},{10,9... | collective-permute-start | bytes 49160 | tf_op jit(solution)/shard_map/ppermute | solution.py:27
  20.0 1.7 %pad.38 = f32[24,160,128]{2,1,0:T(8,128)S(1)} pad(f32[22,160,128]{2,1,0:T(8,128)} %bitcast.74, f32[]{:T(128)} %constant.119.clone.1), padding=0_2x0_0x0_0 | pad | bytes 3768324
  21.7 1.1 %copy.15 = f32[3,8,160,128]{3,1,2,0:T(8,128)S(1)} copy(f32[3,8,160,128]{3,2,1,0:T(8,128)S(1)} %bitcast.73) | data formatting | bytes 3932160
  22.9 36.5 %while.2 = (s32[]{:T(128)}, f32[5,4096]{1,0:T(8,128)S(1)}, s32[5]{0:T(128)S(1)}, f32[22,20480]{1,0:T(8,128)S(1)}, f32[22]{0:T(128)S(1)}, /*index=5*/f32[20480]{0...) while((s32[]{:T(128)}, f32[5,4096]{1,0:T(8,128)S(1)}, ...), condition=%wide.region_1.2_spmd, body=%wide.region_0.1_spmd.sunk | while | flops 235597824 | bytes 7335435 | solution.py:79
  24.3 3.4 %fusion.106 = f32[206,4096]{1,0:T(8,128)S(1)} fusion(f32[206,22]{0,1:T(8,128)S(1)} %get-tuple-element.266, f32[4096]{0:T(1024)S(1)} %get-tuple-element.230, f32[206]{0:T(256)S(1)} %get-tuple-element.268, f32[206]{0:T(256)S(1)} %get-tuple-element.267, f32[22,20480]{1,0:T(8,128)S(1)} %get-tuple-element.263, s32[]{:T(128)S(6)} %select_n.110, ...), kind=kOutput, calls=%fused_computation.3.clone.1 | convolution fusion | flops 225468416 | bytes 3828228 | tf_op jit(solution)/shard_map/while/body/eval_jaxpr/dot_general | solution.py:40
  27.7 2.2 %fusion.107 = f32[1,4096]{1,0:T(1,128)S(1)} fusion(f32[206,4096]{1,0:T(8,128)S(1)} %fusion.106, f32[206,1]{0,1:T(1,128)S(1)} %bitcast.95), kind=kOutput, calls=%fused_computation.154.clone.1 | convolution fusion | flops 10125312 | bytes 3392312 | tf_op jit(solution)/shard_map/while/body/eval_jaxpr/dot_general | solution.py:44
  31.6 3.4 %fusion.106 = f32[206,4096]{1,0:T(8,128)S(1)} fusion(f32[206,22]{0,1:T(8,128)S(1)} %get-tuple-element.266, f32[4096]{0:T(1024)S(1)} %get-tuple-element.230, f32[206]{0:T(256)S(1)} %get-tuple-element.268, f32[206]{0:T(256)S(1)} %get-tuple-element.267, f32[22,20480]{1,0:T(8,128)S(1)} %get-tuple-element.263, s32[]{:T(128)S(6)} %select_n.110, ...), kind=kOutput, calls=%fused_computation.3.clone.1 | convolution fusion | flops 225468416 | bytes 3828228 | tf_op jit(solution)/shard_map/while/body/eval_jaxpr/dot_general | solution.py:40
  35.0 2.2 %fusion.107 = f32[1,4096]{1,0:T(1,128)S(1)} fusion(f32[206,4096]{1,0:T(8,128)S(1)} %fusion.106, f32[206,1]{0,1:T(1,128)S(1)} %bitcast.95), kind=kOutput, calls=%fused_computation.154.clone.1 | convolution fusion | flops 10125312 | bytes 3392312 | tf_op jit(solution)/shard_map/while/body/eval_jaxpr/dot_general | solution.py:44
  38.9 3.3 %fusion.106 = f32[206,4096]{1,0:T(8,128)S(1)} fusion(f32[206,22]{0,1:T(8,128)S(1)} %get-tuple-element.266, f32[4096]{0:T(1024)S(1)} %get-tuple-element.230, f32[206]{0:T(256)S(1)} %get-tuple-element.268, f32[206]{0:T(256)S(1)} %get-tuple-element.267, f32[22,20480]{1,0:T(8,128)S(1)} %get-tuple-element.263, s32[]{:T(128)S(6)} %select_n.110, ...), kind=kOutput, calls=%fused_computation.3.clone.1 | convolution fusion | flops 225468416 | bytes 3828228 | tf_op jit(solution)/shard_map/while/body/eval_jaxpr/dot_general | solution.py:40
  42.3 2.2 %fusion.107 = f32[1,4096]{1,0:T(1,128)S(1)} fusion(f32[206,4096]{1,0:T(8,128)S(1)} %fusion.106, f32[206,1]{0,1:T(1,128)S(1)} %bitcast.95), kind=kOutput, calls=%fused_computation.154.clone.1 | convolution fusion | flops 10125312 | bytes 3392312 | tf_op jit(solution)/shard_map/while/body/eval_jaxpr/dot_general | solution.py:44
  46.2 3.3 %fusion.106 = f32[206,4096]{1,0:T(8,128)S(1)} fusion(f32[206,22]{0,1:T(8,128)S(1)} %get-tuple-element.266, f32[4096]{0:T(1024)S(1)} %get-tuple-element.230, f32[206]{0:T(256)S(1)} %get-tuple-element.268, f32[206]{0:T(256)S(1)} %get-tuple-element.267, f32[22,20480]{1,0:T(8,128)S(1)} %get-tuple-element.263, s32[]{:T(128)S(6)} %select_n.110, ...), kind=kOutput, calls=%fused_computation.3.clone.1 | convolution fusion | flops 225468416 | bytes 3828228 | tf_op jit(solution)/shard_map/while/body/eval_jaxpr/dot_general | solution.py:40
  49.6 2.2 %fusion.107 = f32[1,4096]{1,0:T(1,128)S(1)} fusion(f32[206,4096]{1,0:T(8,128)S(1)} %fusion.106, f32[206,1]{0,1:T(1,128)S(1)} %bitcast.95), kind=kOutput, calls=%fused_computation.154.clone.1 | convolution fusion | flops 10125312 | bytes 3392312 | tf_op jit(solution)/shard_map/while/body/eval_jaxpr/dot_general | solution.py:44
  53.5 3.3 %fusion.106 = f32[206,4096]{1,0:T(8,128)S(1)} fusion(f32[206,22]{0,1:T(8,128)S(1)} %get-tuple-element.266, f32[4096]{0:T(1024)S(1)} %get-tuple-element.230, f32[206]{0:T(256)S(1)} %get-tuple-element.268, f32[206]{0:T(256)S(1)} %get-tuple-element.267, f32[22,20480]{1,0:T(8,128)S(1)} %get-tuple-element.263, s32[]{:T(128)S(6)} %select_n.110, ...), kind=kOutput, calls=%fused_computation.3.clone.1 | convolution fusion | flops 225468416 | bytes 3828228 | tf_op jit(solution)/shard_map/while/body/eval_jaxpr/dot_general | solution.py:40
  56.9 2.2 %fusion.107 = f32[1,4096]{1,0:T(1,128)S(1)} fusion(f32[206,4096]{1,0:T(8,128)S(1)} %fusion.106, f32[206,1]{0,1:T(1,128)S(1)} %bitcast.95), kind=kOutput, calls=%fused_computation.154.clone.1 | convolution fusion | flops 10125312 | bytes 3392312 | tf_op jit(solution)/shard_map/while/body/eval_jaxpr/dot_general | solution.py:44
  60.2 3.7 %all-to-all-start.1 = ((f32[16,1,192]{2,1,0:T(1,128)}), f32[16,1,192]{2,1,0:T(1,128)S(1)}, u32[]{:S(2)}, u32[]{:S(2)}) async-start(f32[16,1,192]{2,1,0:T(1,128)} %reshape.387), calls=%async_computation.1 | async-start | bytes 32768 | tf_op jit(solution)/shard_map/all_to_all | solution.py:209
  64.1 6.1 %all-to-all-done.1 = f32[16,1,192]{2,1,0:T(1,128)S(1)} async-done(((f32[16,1,192]{2,1,0:T(1,128)}), f32[16,1,192]{2,1,0:T(1,128)S(1)}, u32[]{:S(2)}, u32[]{:S(2)}) %all-to-all-start.1) | async-done | bytes 12320 | tf_op jit(solution)/shard_map/all_to_all | solution.py:209
  73.6 3.3 %fusion.11 = f32[206,4096]{1,0:T(8,128)S(1)} fusion(f32[4096]{0:T(1024)S(1)} %bitcast.93, f32[206]{0:T(256)S(1)} %get-tuple-element.288, f32[206]{0:T(256)S(1)} %get-tuple-element.287, f32[22,4096]{1,0:T(8,128)S(1)} %bitcast.82, f32[4096]{0:T(1024)S(1)} %bitcast_log_fusion, f32[22]{0:T(128)S(1)} %get-tuple-element.289, s32[206,22]{0,1:T(8,128)S(1)} %copy-done.2), kind=kOutput, calls=%fused_computation.13 | convolution fusion | flops 225482016 | bytes 3788184 | tf_op jit(solution)/shard_map/while/body/eval_jaxpr/dot_general | solution.py:40
  76.9 1.7 %fusion.67 = f32[1,4096]{1,0:T(1,128)S(1)} fusion(f32[206,4096]{1,0:T(8,128)S(1)} %fusion.11, f32[1,206]{1,0:T(1,128)S(1)} %bitcast.96), kind=kOutput, calls=%fused_computation.131 | convolution fusion | flops 10125312 | bytes 3392312 | tf_op jit(solution)/shard_map/while/body/eval_jaxpr/dot_general | solution.py:44
  78.6 2.9 %multiply_reduce_fusion = f32[4,1024]{1,0:T(4,128)S(1)} fusion(f32[192,1024]{1,0:T(8,128)S(1)} %bitcast.79, f32[1,192,128]{2,1,0:T(8,128)S(1)} %bitcast.91, f32[1,192,128]{2,1,0:T(8,128)S(1)} %bitcast.89, f32[1,192,128]{2,1,0:T(8,128)S(1)} %bitcast.90, f32[1,192,128]{2,1,0:T(8,128)S(1)} %bitcast.83, f32[1024]{0:T(1024)S(1)} %squeeze.25, ...), kind=kOutput, calls=%fused_computation.14 | convolution fusion | flops 1210478592 | bytes 1212416 | tf_op jit(solution)/shard_map/while/body/eval_jaxpr/dot_general | solution.py:135
  82.3 3.5 %all-to-all-start.2 = ((f32[16,1,256]{2,1,0:T(1,128)}), f32[16,1,256]{2,1,0:T(1,128)S(1)}, u32[]{:S(2)}, u32[]{:S(2)}) async-start(f32[16,1,256]{2,1,0:T(1,128)} %reshape.389), calls=%async_computation.2 | async-start | bytes 32768 | tf_op jit(solution)/shard_map/all_to_all | solution.py:217
  85.9 6.4 %all-to-all-done.2 = f32[16,1,256]{2,1,0:T(1,128)S(1)} async-done(((f32[16,1,256]{2,1,0:T(1,128)}), f32[16,1,256]{2,1,0:T(1,128)S(1)}, u32[]{:S(2)}, u32[]{:S(2)}) %all-to-all-start.2) | async-done | bytes 16416 | tf_op jit(solution)/shard_map/all_to_all | solution.py:217
  (104 shorter events, 17.2 us)
Async XLA Ops:
  0.0 19.1 %copy-start = (f32[22]{0:T(128)S(1)}, f32[22]{0:T(128)}, u32[]{:S(2)}) copy-start(f32[22]{0:T(128)} %param.17) | copy-start | bytes 268
  0.0 71.8 %collective-permute-start.2 = (f32[5,32,128]{2,1,0:T(8,128)}, f32[5,32,128]{2,1,0:T(8,128)S(1)}, u32[]{:S(2)}, u32[]{:S(2)}) collective-permute-start(f32[5,32,128]{2,1,0:T(8,128)} %param.15), channel_id=1, source_target_pairs={{0,1},{1,2},{2,3},{3,4},{4,5},{5,6},{6,7},{7,8},{8,9},{9,10},{10,1... | collective-permute-start | bytes 245768 | tf_op jit(solution)/shard_map/ppermute | solution.py:19
  0.5 71.3 %collective-permute-start.1 = (f32[5,32,128]{2,1,0:T(8,128)}, f32[5,32,128]{2,1,0:T(8,128)S(1)}, u32[]{:S(2)}, u32[]{:S(2)}) collective-permute-start(f32[5,32,128]{2,1,0:T(8,128)} %param.15), channel_id=1, source_target_pairs={{1,0},{2,1},{3,2},{4,3},{5,4},{6,5},{7,6},{8,7},{9,8},{10,9},{11,1... | collective-permute-start | bytes 245768 | tf_op jit(solution)/shard_map/ppermute | solution.py:20
  6.8 53.3 %all-to-all-start = ((f32[16,1,64]{2,1,0:T(1,128)}), f32[16,1,64]{2,1,0:T(1,128)S(1)}, u32[]{:S(2)}, u32[]{:S(2)}) async-start(f32[16,1,64]{2,1,0:T(1,128)} %bitcast.17), calls=%async_computation | async-start | bytes 16384 | tf_op jit(solution)/shard_map/all_to_all | solution.py:208
  11.2 52.8 %collective-permute-start = (f32[1,32,128]{2,1,0:T(8,128)S(1)}, f32[1,32,128]{2,1,0:T(8,128)S(1)}, u32[]{:S(2)}, u32[]{:S(2)}) collective-permute-start(f32[1,32,128]{2,1,0:T(8,128)S(1)} %slice.218), channel_id=1, source_target_pairs={{0,15},{1,0},{2,1},{3,2},{4,3},{5,4},{6,5},{7,6},{8,7},{9,8},{10,9... | collective-permute-start | bytes 49160 | tf_op jit(solution)/shard_map/ppermute | solution.py:27
  16.6 56.7 %collective-permute-start.3 = (f32[22,1,32,128]{3,2,1,0:T(8,128)S(1)}, f32[22,1,32,128]{3,2,1,0:T(8,128)S(1)}, u32[]{:S(2)}, u32[]{:S(2)}) collective-permute-start(f32[22,1,32,128]{3,2,1,0:T(8,128)S(1)} %slice.260), channel_id=1, source_target_pairs={{0,15},{1,0},{2,1},{3,2},{4,3},{5,4},{6,5},{7,6},{8,7},{9,8},{10,9... | collective-permute-start | bytes 1081352 | tf_op jit(solution)/shard_map/ppermute | solution.py:27
  20.0 2.9 %copy-start.1 = (f32[5,32,128]{2,1,0:T(8,128)S(1)}, f32[5,32,128]{2,1,0:T(8,128)}, u32[]{:S(2)}) copy-start(f32[5,32,128]{2,1,0:T(8,128)} %param.14) | copy-start | bytes 245764
  20.0 2.9 %copy-start.6 = (f32[206]{0:T(256)S(1)}, f32[206]{0:T(256)}, u32[]{:S(2)}) copy-start(f32[206]{0:T(256)} %param.19) | copy-start | bytes 2476
  22.9 36.5 %copy-start.4 = (f32[1,16,3,64]{3,1,2,0:T(8,128)S(1)}, f32[1,16,3,64]{3,1,2,0:T(8,128)}, u32[]{:S(2)}) copy-start(f32[1,16,3,64]{3,1,2,0:T(8,128)} %param.22) | copy-start | bytes 36868
  22.9 48.9 %copy-start.3 = (f32[5,32,128]{2,1,0:T(8,128)S(1)}, f32[5,32,128]{2,1,0:T(8,128)}, u32[]{:S(2)}) copy-start(f32[5,32,128]{2,1,0:T(8,128)} %param.15) | copy-start | bytes 245764
  60.2 10.0 %all-to-all-start.1 = ((f32[16,1,192]{2,1,0:T(1,128)}), f32[16,1,192]{2,1,0:T(1,128)S(1)}, u32[]{:S(2)}, u32[]{:S(2)}) async-start(f32[16,1,192]{2,1,0:T(1,128)} %reshape.387), calls=%async_computation.1 | async-start | bytes 32768 | tf_op jit(solution)/shard_map/all_to_all | solution.py:209
  72.6 1.0 %copy-start.2 = (s32[206,22]{0,1:T(8,128)S(1)}, s32[206,22]{0,1:T(8,128)}, u32[]{:S(2)}) copy-start(s32[206,22]{0,1:T(8,128)} %param.20) | copy-start | bytes 54388
  76.9 8.9 %copy-start.5 = (s32[1,16]{1,0:T(1,128)S(1)}, s32[1,16]{1,0:T(1,128)}, u32[]{:S(2)}) copy-start(s32[1,16]{1,0:T(1,128)} %param.23) | copy-start | bytes 196
  82.3 10.0 %all-to-all-start.2 = ((f32[16,1,256]{2,1,0:T(1,128)}), f32[16,1,256]{2,1,0:T(1,128)S(1)}, u32[]{:S(2)}, u32[]{:S(2)}) async-start(f32[16,1,256]{2,1,0:T(1,128)} %reshape.389), calls=%async_computation.2 | async-start | bytes 32768 | tf_op jit(solution)/shard_map/all_to_all | solution.py:217
where the time goes:
time: 94.2 us; the launch traced here: 93.6 us
  matrix products  36.3 us (39%)
  starting transfers between devices  21.1 us (22%)
  local copies, waits for them, and re-layouts  14.9 us (16%)
  waiting for transfers between devices  12.5 us (13%)
  other arithmetic  4.59 us (5%)
  loops' own time  3.68 us (4%)
    dot_general x6, matrix products, heat_block(): jnp.dot(kinetic_exponents, log_conc, precision=highest_precision, preferr...  20.1 us
    dot_general x6, matrix products, heat_block(): jnp.dot(combined_thermal_output, jnp.exp(log_rate), precision=highest_pre...  12.5 us
    all_to_all x1, waiting for transfers between devices, local(): lax.all_to_all(sampled, 'gx', split_axis=0, concat_axis=0, tiled=True)  6.38 us
    all_to_all x1, waiting for transfers between devices, local(): lax.all_to_all(outgoing[1], 'gx', split_axis=0, concat_axis=0, tiled=True)  6.11 us
    ppermute x1, starting transfers between devices, with_halo(): after = lax.ppermute(first, axis, down)  5.04 us
    unnamed x28, local copies, waits for them, and re-layouts  4.84 us
    ppermute x2, starting transfers between devices, from_behind(): return lax.ppermute(x, axis, [(i, (i + by) % count) for i in range(count)])  4.79 us
    all_to_all x1, starting transfers between devices, local(): lax.all_to_all(outgoing[1], 'gx', split_axis=0, concat_axis=0, tiled=True)  3.69 us
  transfers between devices with their start and end apart: 7, of which 2 were waited for; matrix products, arithmetic and copies ran while one was open for 49% of the time, Pallas kernels for 0%

commit v1 on v0

v1 whole, which is shorter than its diff:
```python
import functools

import jax
import jax.numpy as jnp
from jax import lax
from jax.experimental import pallas as pl
from jax.experimental.pallas import tpu as pltpu
from jax.sharding import PartitionSpec as P

stencil_coeffs = (0.8, -0.2, 4.0 / 105.0, -1.0 / 280.0)
reach = 4
log2e = 1.4426950408889634
MESH = pl.DeviceIdType.MESH
f32 = jnp.float32
bf16 = jnp.bfloat16


def split3(x):
    hi = x.astype(bf16)
    rest = x - hi.astype(f32)
    mid = rest.astype(bf16)
    lo = (rest - mid.astype(f32)).astype(bf16)
    return hi, mid, lo


def split2(x):
    hi = x.astype(bf16)
    return hi, (x - hi.astype(f32)).astype(bf16)


def kernel(
    n,
    species_hbm,
    t_ref,
    fuel_ref,
    par_ref,
    stoich_ref,
    pos_ref,
    off_ref,
    out_ref,
    species,
    feat,
    weights,
    heat_weight,
    heat,
    fcat,
    halo_before,
    halo_after,
    edge_t,
    edge_out,
    edge_in,
    pack,
    recv,
    back,
    home,
    load_sem,
    halo_send,
    halo_recv,
    out_send,
    out_recv,
    home_send,
    home_recv,
):
    me = lax.axis_index("gx")
    nxt, prv = lax.rem(me + 1, n), lax.rem(me + n - 1, n)
    n_species, planes, ny, nz = species_hbm.shape
    slots = pos_ref.shape[1]
    reactions = stoich_ref.shape[0]
    padded = weights.shape[0]
    group = 32

    loads = [
        pltpu.make_async_copy(species_hbm.at[:, p], species.at[p], load_sem.at[p])
        for p in range(planes)
    ]
    for copy in loads:
        copy.start()

    barrier = pltpu.get_barrier_semaphore()

    def greet(k, _):
        pl.semaphore_signal(
            barrier, inc=1, device_id={"gx": lax.rem(me + k, n)}, device_id_type=MESH
        )
        return 0

    lax.fori_loop(1, n, greet, 0)

    def pack_one(d, _):
        pack[d, 0:1, 0:slots] = pos_ref[pl.ds(d, 1), :].astype(f32)
        pack[d, 1:4, 0:slots] = off_ref[d]
        return 0

    lax.fori_loop(0, n, pack_one, 0)

    lane = lax.broadcasted_iota(jnp.int32, (padded, 128), 1)
    stoich = jnp.zeros((padded, 128), f32)
    weights_f = jnp.zeros((padded, 128), f32)
    heat_weight[...] = jnp.zeros_like(heat_weight)
    feat_rows = jnp.zeros((ny, nz), f32)
    stoich_pad = heat_weight
    stoich_pad[0:reactions, 0:n_species] = stoich_ref[...].astype(f32)
    stoich = stoich_pad[...]
    orders = jnp.maximum(-stoich, 0.0)
    par = par_ref[...]
    net = -jnp.sum(stoich * par[3:4, 0:128], axis=1, keepdims=True)
    mass_term = jnp.sum(orders * jnp.log(par[2:3, 0:128]), axis=1, keepdims=True)
    columns = jnp.transpose(
        jnp.concatenate([jnp.log(par[0:1]), par[1:2], jnp.zeros((126, 256), f32)], axis=0)
    )[0:padded]
    offset = (columns[:, 0:1] - mass_term) * log2e
    barrier_col = columns[:, 1:2] * (-log2e)
    in_group = lane % group
    live_lane = lane < 3 * group
    weights_f = orders + pltpu.roll(orders, group, 1) + pltpu.roll(orders, 2 * group, 1)
    for j, part in enumerate(split3(barrier_col)):
        weights_f = jnp.where(in_group == n_species + j, part.astype(f32), weights_f)
    for j, part in enumerate(split3(offset)):
        weights_f = jnp.where(in_group == n_species + 3 + j, part.astype(f32), weights_f)
    weights[...] = jnp.where(live_lane, weights_f, 0.0).astype(bf16)
    heat_weight[...] = jnp.broadcast_to(net, heat_weight.shape)

    ones = jnp.ones((ny, nz), f32)
    for j in range(3):
        feat[(n_species + 3 + j) * ny : (n_species + 4 + j) * ny, :] = ones
    for j in range(n_species + 6, group):
        feat[j * ny : (j + 1) * ny, :] = jnp.zeros((ny, nz), f32)

    batch = 8

    def heat_plane(p):
        loads[p].wait()
        temper = t_ref[p]
        log_t = jnp.log(temper)
        for s in range(n_species):
            feat[s * ny : (s + 1) * ny, :] = (jnp.log(species[p, s]) - log_t) * log2e
        inverse = 1.0 / temper
        for j in range(3):
            feat[(n_species + j) * ny : (n_species + j + 1) * ny, :] = inverse

        def rows(i, _):
            for b in range(0, batch, 2):
                r = i * batch + b
                f = jnp.concatenate(
                    [
                        feat[pl.ds(r, group, stride=ny), :],
                        feat[pl.ds(r + 1, group, stride=ny), :],
                    ],
                    axis=1,
                )
                x = jnp.dot(
                    weights[:, 0 : 3 * group],
                    jnp.concatenate(split3(f), axis=0),
                    preferred_element_type=f32,
                )
                rate = jnp.exp2(x)
                hw = heat_weight[...]
                for h in range(2):
                    term = rate[:, h * 128 : (h + 1) * 128] * hw
                    total = jnp.sum(term.reshape(padded // 8, 8, 128), axis=0)
                    heat[pl.ds(p * ny + r + h, 1), :] = jnp.sum(total, axis=0, keepdims=True)
            return 0

        lax.fori_loop(0, ny // batch, rows, 0)

    def put(p, f, value):
        hi, lo = split2(value)
        r = (p * 4 + f) * ny
        fcat[r : r + ny, 0:nz] = hi
        fcat[r : r + ny, nz : 2 * nz] = lo

    def plane_of(q):
        if q < 0:
            return halo_before[q + reach]
        if q >= planes:
            return halo_after[q - planes]
        return fuel_ref[q]

    def dissip(p):
        centre = plane_of(p)
        gx = jnp.zeros_like(centre)
        gy = jnp.zeros_like(centre)
        gz = jnp.zeros_like(centre)
        for k in range(1, reach + 1):
            c = stencil_coeffs[k - 1]
            gx = gx + c * (plane_of(p + k) - plane_of(p - k))
            gy = gy + c * (pltpu.roll(centre, ny - k, 0) - pltpu.roll(centre, k, 0))
            gz = gz + c * (pltpu.roll(centre, nz - k, 1) - pltpu.roll(centre, k, 1))
        return jnp.exp(0.7 * jnp.log(t_ref[p])) * (gx * gx + gy * gy + gz * gz)

    def remote(src, dst, send, got, to):
        return pltpu.make_async_remote_copy(
            src_ref=src,
            dst_ref=dst,
            send_sem=send,
            recv_sem=got,
            device_id={"gx": to},
            device_id_type=MESH,
        )

    heat_plane(0)

    pl.semaphore_wait(barrier, n - 1)
    up = remote(
        fuel_ref.at[pl.ds(planes - reach, reach)], halo_before, halo_send.at[0], halo_recv.at[0], nxt
    )
    down = remote(fuel_ref.at[pl.ds(0, reach)], halo_after, halo_send.at[1], halo_recv.at[1], prv)
    down_t = remote(t_ref.at[0], edge_t, halo_send.at[2], halo_recv.at[2], prv)
    down_e = remote(edge_out, edge_in, halo_send.at[3], halo_recv.at[3], prv)
    up.start()

    def send_out(k, _):
        d = lax.rem(me + k, n)
        remote(pack.at[d], recv.at[me], out_send.at[d], out_recv.at[me], d).start()
        return 0

    lax.fori_loop(1, n, send_out, 0)
    down.start()
    down_t.start()
    recv[me] = pack[me]

    heat_plane(1)
    up.wait_recv()
    first = dissip(0)
    edge_out[0] = first
    edge_out[1] = heat[0:ny, :]
    for p in range(2, planes):
        heat_plane(p)
        if p == 2:
            down_e.start()
    down.wait_recv()
    for p in range(planes):
        put(p, 0, t_ref[p])
        put(p, 1, fuel_ref[p])
        put(p, 2, first if p == 0 else dissip(p))
        put(p, 3, heat[p * ny : (p + 1) * ny, :])
    down_t.wait_recv()
    down_e.wait_recv()
    put(planes, 0, edge_t[...])
    put(planes, 1, halo_after[0])
    put(planes, 2, edge_in[0])
    put(planes, 3, edge_in[1])

    def got_one(k, _):
        d = lax.rem(me + k, n)
        remote(pack.at[d], recv.at[d], out_send.at[d], out_recv.at[d], d).wait()
        return 0

    lax.fori_loop(1, n, got_one, 0)

    low = lax.broadcasted_iota(jnp.int32, (4, 128), 1) < slots
    z_label = lax.broadcasted_iota(jnp.int32, (nz, 256), 0).astype(f32)
    y_label = lax.broadcasted_iota(jnp.int32, (ny, 256), 0).astype(f32)

    def sample(g, _):
        halves = [
            jnp.where(low, recv[4 * g + 2 * h], pltpu.roll(recv[4 * g + 2 * h + 1], slots, 1))
            for h in range(2)
        ]
        t = jnp.concatenate(halves, axis=1)
        cell, fx, fy, fz = (t[i : i + 1] for i in range(4))
        cx = jnp.floor((cell + 0.5) * (1.0 / (ny * nz)))
        cell = cell - cx * (ny * nz)
        cy = jnp.floor((cell + 0.5) * (1.0 / nz))
        cz = cell - cy * nz
        cy1 = jnp.where(cy + 1.0 >= ny, 0.0, cy + 1.0)
        cz1 = jnp.where(cz + 1.0 >= nz, 0.0, cz + 1.0)
        wz = jnp.where(z_label == cz, 1.0 - fz, jnp.where(z_label == cz1, fz, 0.0))
        wy = jnp.where(y_label == cy, 1.0 - fy, jnp.where(y_label == cy1, fy, 0.0))
        wh, wl = split2(wz)
        both = jnp.concatenate([wh, wh], axis=0)
        acc = jnp.zeros((4, 8, 256), f32)
        for p in range(planes + 1):
            rows = slice(p * 4 * ny, (p + 1) * 4 * ny)
            a = jnp.dot(fcat[rows, :], both, preferred_element_type=f32)
            a = a + jnp.dot(fcat[rows, 0:nz], wl, preferred_element_type=f32)
            wx = jnp.where(cx == p, 1.0 - fx, jnp.where(cx == p - 1.0, fx, 0.0))
            a = a.reshape(4, ny // 8, 8, 256) * wy.reshape(ny // 8, 8, 256)[None]
            acc = acc + jnp.sum(a, axis=1) * wx.reshape(1, 1, 256)
        v = jnp.sum(acc, axis=1)
        for j in range(4):
            s = 4 * g + j
            block = v[:, (j // 2) * 128 : (j // 2 + 1) * 128]
            if j % 2:
                block = pltpu.roll(block, 128 - slots, 1)
            back[s] = block

            @pl.when(s != me)
            def _():
                remote(back.at[s], home.at[me], home_send.at[s], home_recv.at[me], s).start()

        return 0

    lax.fori_loop(0, n // 4, sample, 0)
    home[me] = back[me]

    def home_one(k, _):
        d = lax.rem(me + k, n)
        remote(back.at[d], home.at[d], home_send.at[d], home_recv.at[d], d).wait()
        return 0

    lax.fori_loop(1, n, home_one, 0)
    for copy in (up, down, down_t, down_e):
        copy.wait_send()
    out_ref[...] = home[...]


def local(
    component_shares,
    thermal_ratio,
    fuel_share,
    species_mass_unit,
    formation_energy,
    frequency_factor,
    arrhenius_barrier,
    product_minus_reactant,
    particle_voxel_position,
    particle_voxel_offset,
    particle_active_total,
):
    n = lax.axis_size("gx")
    n_species, planes, ny, nz = component_shares.shape
    reactions = frequency_factor.shape[0]
    slots = particle_voxel_position.shape[2]
    padded = (reactions + 7) // 8 * 8
    fill = lambda a, v: jnp.pad(a, (0, 256 - a.shape[0]), constant_values=v)
    par = jnp.stack(
        [
            fill(frequency_factor, 1.0),
            fill(arrhenius_barrier, 0.0),
            fill(species_mass_unit, 1.0),
            fill(formation_energy, 0.0),
        ]
    )
    vmem = pl.BlockSpec(memory_space=pltpu.VMEM)
    dma = pltpu.SemaphoreType.DMA
    returned = pl.pallas_call(
        functools.partial(kernel, n),
        out_shape=jax.ShapeDtypeStruct((n, 4, 128), f32),
        in_specs=[pl.BlockSpec(memory_space=pl.ANY)] + [vmem] * 6,
        out_specs=vmem,
        scratch_shapes=[
            pltpu.VMEM((planes, n_species, ny, nz), f32),
            pltpu.VMEM((32 * ny, nz), f32),
            pltpu.VMEM((padded, 128), bf16),
            pltpu.VMEM((padded, 128), f32),
            pltpu.VMEM((planes * ny, nz), f32),
            pltpu.VMEM(((planes + 1) * 4 * ny, 2 * nz), bf16),
            pltpu.VMEM((reach, ny, nz), f32),
            pltpu.VMEM((reach, ny, nz), f32),
            pltpu.VMEM((ny, nz), f32),
            pltpu.VMEM((2, ny, nz), f32),
            pltpu.VMEM((2, ny, nz), f32),
            pltpu.VMEM((n, 4, 128), f32),
            pltpu.VMEM((n, 4, 128), f32),
            pltpu.VMEM((n, 4, 128), f32),
            pltpu.VMEM((n, 4, 128), f32),
            dma((planes,)),
            dma((4,)),
            dma((4,)),
            dma((n,)),
            dma((n,)),
            dma((n,)),
            dma((n,)),
        ],
        compiler_params=pltpu.CompilerParams(collective_id=0, has_side_effects=True),
    )(
        component_shares,
        thermal_ratio,
        fuel_share,
        par,
        product_minus_reactant,
        particle_voxel_position[0],
        particle_voxel_offset[0],
    )
    live_slot = jnp.arange(slots, dtype=jnp.int32)[None, :] < particle_active_total[0][:, None]
    return jnp.where(live_slot[:, None, :], returned[:, :, 0:slots], f32(0.0))[None]


def solution(mesh):
    placed = (
        P(None, ("snap", "gx"), None, None),
        P(("snap", "gx"), None, None),
        P(("snap", "gx"), None, None),
        P(),
        P(),
        P(),
        P(),
        P(),
        P(("snap", "gx"), None, None),
        P(("snap", "gx"), None, None, None),
        P(("snap", "gx"), None),
    )
    return jax.shard_map(
        local,
        mesh=mesh,
        in_specs=placed,
        out_specs=P(("snap", "gx"), None, None, None),
        check_vma=False,
    )
```

time: 94.2 us -> 29.5 us (0.31)
  matrix products: 36.3 us -> 0 us
  Pallas kernels: 0 us -> 21.5 us
  starting transfers between devices: 21.1 us -> 0 us
  waiting for transfers between devices: 12.5 us -> 0 us
  local copies, waits for them, and re-layouts: 14.9 us -> 5.54 us
  loops' own time: 3.68 us -> 0 us
  other arithmetic: 4.59 us -> 2.06 us
    dot_general x14 -> x0, matrix products: 36.3 us -> none  [the longest x6 20.1 us: heat_block(): jnp.dot(kinetic_exponents, log_conc, precision=highest_precision, preferr...]
    pallas_call x0 -> x1, Pallas kernels: none -> 21.5 us  [local(): pl.pallas_call(functools.partial(kernel, n), out_shape=jax.ShapeDtypeStru...]
    all_to_all x3 -> x0, waiting for transfers between devices: 12.5 us -> none  [the longest x1 6.38 us: local(): lax.all_to_all(sampled, 'gx', split_axis=0, concat_axis=0, tiled=True)]
    all_to_all x3 -> x0, starting transfers between devices: 10.8 us -> none  [the longest x1 3.69 us: local(): lax.all_to_all(outgoing[1], 'gx', split_axis=0, concat_axis=0, tiled=True)]
    ppermute x4 -> x0, starting transfers between devices: 10.3 us -> none  [the longest x1 5.04 us: with_halo(): after = lax.ppermute(first, axis, down)]
    another operation x1 -> x0, loops' own time: 3.68 us -> none  [thermal_output_grid(): lax.map(thermal_one_block, jnp.arange(blocks, dtype=jnp.int32))]
    dynamic_slice x5 -> x0, local copies, waits for them, and re-layouts: 3.32 us -> none  [thermal_output_grid(): lax.map(thermal_one_block, jnp.arange(blocks, dtype=jnp.int32))]
    pad x0 -> x4, local copies, waits for them, and re-layouts: none -> 2.68 us  [local(): fill = lambda a, v: jnp.pad(a, (0, 256 - a.shape[0]), constant_values=v)]
  transfers between devices with their start and end apart: 7 -> 0, of which waited for: 2 -> 0; matrix products, arithmetic and copies ran while one was open for 49% -> 0% of each run, Pallas kernels for 0% -> 0%
where the time goes in v1:
time: 29.5 us; the launch traced here: 29.1 us
  Pallas kernels  21.5 us (73%)
  local copies, waits for them, and re-layouts  5.54 us (19%)
  other arithmetic  2.06 us (7%)
    pallas_call x1, Pallas kernels, local(): pl.pallas_call(functools.partial(kernel, n), out_shape=jax.ShapeDtypeStru...  21.5 us
    unnamed x4, local copies, waits for them, and re-layouts  2.86 us
    pad x4, local copies, waits for them, and re-layouts, local(): fill = lambda a, v: jnp.pad(a, (0, 256 - a.shape[0]), constant_values=v)  2.68 us
    broadcast_in_dim x1, other arithmetic, local(): jnp.where(live_slot[:, None, :], returned[:, :, 0:slots], f32(0.0))[None]  1.39 us
    another operation x1, other arithmetic, local(): jnp.stack([fill(frequency_factor, 1.0), fill(arrhenius_barrier, 0.0), fil...  0.6 us

profile of v1, /device:TPU:0, one launch (start us, length us, event | category | flops | bytes accessed | tf_op | source)
XLA Modules:
  0.0 29.1 jit_solution(6346662919500392368)
XLA Ops:
  0.0 0.0 copy-start
  0.0 1.5 %copy.13.stoich_ref = s32[206,22]{1,0:T(8,128)} copy(s32[206,22]{0,1:T(8,128)} %param.18) | data formatting | bytes 36256 | tf_op args[7]
  1.5 1.4 %copy.15 = f32[1,16,3,64]{3,2,1,0:T(4,128)} copy(f32[1,16,3,64]{3,1,2,0:T(8,128)} %param.20) | data formatting | bytes 24576 | tf_op args[9]
  2.9 0.7 %pad.14 = f32[256]{0:T(256)S(1)} pad(f32[206]{0:T(256)} %param.16, f32[]{:T(128)} %constant.0.clone.1), padding=0_50 | pad | bytes 1852 | tf_op jit(solution)/shard_map/jit(_pad)/pad | solution.py:326
  3.5 0.7 %pad.15 = f32[256]{0:T(256)S(1)} pad(f32[206]{0:T(256)} %param.17, f32[]{:T(128)} %constant.1.clone.1), padding=0_50 | pad | bytes 1852 | tf_op jit(solution)/shard_map/jit(_pad)/pad | solution.py:326
  4.2 0.7 %pad.16 = f32[256]{0:T(256)S(1)} pad(f32[22]{0:T(128)} %param.14, f32[]{:T(128)} %constant.0.clone.1), padding=0_234 | pad | bytes 1116 | tf_op jit(solution)/shard_map/jit(_pad)/pad | solution.py:326
  4.9 0.7 %pad.17 = f32[256]{0:T(256)S(1)} pad(f32[22]{0:T(128)} %param.15, f32[]{:T(128)} %constant.1.clone.1), padding=0_234 | pad | bytes 1116 | tf_op jit(solution)/shard_map/jit(_pad)/pad | solution.py:326
  5.5 0.6 %pad_maximum_fusion.par_ref = f32[4,256]{1,0:T(4,128)} fusion(f32[1,256]{1,0:T(1,128)S(1)} %bitcast.16, f32[1,256]{1,0:T(1,128)S(1)} %bitcast.15, f32[1,256]{1,0:T(1,128)S(1)} %bitcast.14, f32[1,256]{1,0:T(1,128)S(1)} %bitcast.13), kind=kLoop, calls=%fused_computation.3 | loop fusion | flops 3072 | bytes 8192 | tf_op jit(solution)/shard_map/stack | solution.py:327
  6.1 21.5 %shard_map.109 = f32[16,4,128]{2,1,0:T(4,128)} custom-call(f32[22,5,32,128]{3,2,1,0:T(8,128)} %species_hbm.1, f32[5,32,128]{2,1,0:T(8,128)} %t_ref.1, f32[5,32,128]{2,1,0:T(8,128)} %fuel_ref.1, f32[4,256]{1,0:T(4,128)} %pad_maximum_fusion.par_ref, s32[206,22]{1,0:T(8,128)} %copy.13.stoich_ref, s32[16,64]{1,0:T(8,128)} %bitcast.12, f32[16,3,64]{2,1,0:T(4,128)} %bitcast.11), custom_call_target="tpu_custom_call" | custom-call | tf_op jit(solution)/shard_map/pallas_call | solution.py:337
  27.6 0.0 copy-done
  27.6 0.1 iota_compare_fusion
  27.7 1.4 %select_bitcast_fusion = f32[1,16,4,64]{3,2,1,0:T(4,128)} fusion(f32[16,4,128]{2,1,0:T(4,128)} %shard_map.109, pred[16,64]{1,0:T(8,128)(4,1)S(1)} %iota_compare_fusion), kind=kLoop, calls=%fused_computation.1 | loop fusion | flops 4096 | bytes 33792 | tf_op jit(solution)/shard_map/broadcast_in_dim | solution.py:377
Async XLA Ops:
  0.0 27.6 %copy-start = (s32[1,16]{1,0:T(1,128)S(1)}, s32[1,16]{1,0:T(1,128)}, u32[]{:S(2)}) copy-start(s32[1,16]{1,0:T(1,128)} %param.21) | copy-start | bytes 196

commit v2 on v1

--- a/solution.py
+++ b/solution.py
@@ -33,15 +33,20 @@
     species_hbm,
     t_ref,
     fuel_ref,
-    par_ref,
+    mass_ref,
+    formation_ref,
+    frequency_ref,
+    barrier_ref,
     stoich_ref,
     pos_ref,
     off_ref,
+    live_ref,
     out_ref,
     species,
     feat,
     weights,
     heat_weight,
+    table,
     heat,
     fcat,
     halo_before,
@@ -65,7 +70,7 @@
     nxt, prv = lax.rem(me + 1, n), lax.rem(me + n - 1, n)
     n_species, planes, ny, nz = species_hbm.shape
     slots = pos_ref.shape[1]
-    reactions = stoich_ref.shape[0]
+    reactions = stoich_ref.shape[1]
     padded = weights.shape[0]
     group = 32
 
@@ -88,37 +93,36 @@
 
     def pack_one(d, _):
         pack[d, 0:1, 0:slots] = pos_ref[pl.ds(d, 1), :].astype(f32)
-        pack[d, 1:4, 0:slots] = off_ref[d]
+        for i in range(3):
+            pack[d, i + 1 : i + 2, 0:slots] = off_ref[i, pl.ds(d, 1), :]
         return 0
 
     lax.fori_loop(0, n, pack_one, 0)
 
-    lane = lax.broadcasted_iota(jnp.int32, (padded, 128), 1)
-    stoich = jnp.zeros((padded, 128), f32)
-    weights_f = jnp.zeros((padded, 128), f32)
-    heat_weight[...] = jnp.zeros_like(heat_weight)
-    feat_rows = jnp.zeros((ny, nz), f32)
-    stoich_pad = heat_weight
-    stoich_pad[0:reactions, 0:n_species] = stoich_ref[...].astype(f32)
-    stoich = stoich_pad[...]
+    table[...] = jnp.zeros_like(table)
+    stoich = stoich_ref[...].astype(f32)
     orders = jnp.maximum(-stoich, 0.0)
-    par = par_ref[...]
-    net = -jnp.sum(stoich * par[3:4, 0:128], axis=1, keepdims=True)
-    mass_term = jnp.sum(orders * jnp.log(par[2:3, 0:128]), axis=1, keepdims=True)
-    columns = jnp.transpose(
-        jnp.concatenate([jnp.log(par[0:1]), par[1:2], jnp.zeros((126, 256), f32)], axis=0)
-    )[0:padded]
-    offset = (columns[:, 0:1] - mass_term) * log2e
-    barrier_col = columns[:, 1:2] * (-log2e)
-    in_group = lane % group
-    live_lane = lane < 3 * group
-    weights_f = orders + pltpu.roll(orders, group, 1) + pltpu.roll(orders, 2 * group, 1)
-    for j, part in enumerate(split3(barrier_col)):
-        weights_f = jnp.where(in_group == n_species + j, part.astype(f32), weights_f)
-    for j, part in enumerate(split3(offset)):
-        weights_f = jnp.where(in_group == n_species + 3 + j, part.astype(f32), weights_f)
-    weights[...] = jnp.where(live_lane, weights_f, 0.0).astype(bf16)
-    heat_weight[...] = jnp.broadcast_to(net, heat_weight.shape)
+    same = lax.broadcasted_iota(jnp.int32, (n_species, n_species), 0) == lax.broadcasted_iota(
+        jnp.int32, (n_species, n_species), 1
+    )
+    log_mass = jnp.sum(jnp.where(same, jnp.log(mass_ref[...]), 0.0), axis=1, keepdims=True)
+    formation = jnp.sum(jnp.where(same, formation_ref[...], 0.0), axis=1, keepdims=True)
+    net = -jnp.sum(stoich * formation, axis=0, keepdims=True)
+    offset = jnp.log(frequency_ref[...]) - jnp.sum(orders * log_mass, axis=0, keepdims=True)
+    extra = [
+        part.astype(f32)
+        for row in (barrier_ref[...] * (-log2e), offset * log2e)
+        for part in split3(row)
+    ]
+    for j in range(3):
+        table[j * group : j * group + n_species, 0:reactions] = orders
+        for i, row in enumerate(extra):
+            r = j * group + n_species + i
+            table[r : r + 1, 0:reactions] = row
+    table[3 * group : 3 * group + 1, 0:reactions] = net
+    columns = jnp.transpose(table[...])[0:padded]
+    weights[...] = columns.astype(bf16)
+    heat_weight[...] = jnp.broadcast_to(columns[:, 3 * group : 3 * group + 1], (padded, 128))
 
     ones = jnp.ones((ny, nz), f32)
     for j in range(3):
@@ -126,7 +130,7 @@
     for j in range(n_species + 6, group):
         feat[j * ny : (j + 1) * ny, :] = jnp.zeros((ny, nz), f32)
 
-    batch = 8
+    batch = 32
 
     def heat_plane(p):
         loads[p].wait()
@@ -252,7 +256,8 @@
     z_label = lax.broadcasted_iota(jnp.int32, (nz, 256), 0).astype(f32)
     y_label = lax.broadcasted_iota(jnp.int32, (ny, 256), 0).astype(f32)
 
-    def sample(g, _):
+    def sample(step, _):
+        g = lax.rem(me // 4 + 1 + step, n // 4)
         halves = [
             jnp.where(low, recv[4 * g + 2 * h], pltpu.roll(recv[4 * g + 2 * h + 1], slots, 1))
             for h in range(2)
@@ -302,7 +307,14 @@
     lax.fori_loop(1, n, home_one, 0)
     for copy in (up, down, down_t, down_e):
         copy.wait_send()
-    out_ref[...] = home[...]
+
+    slot = lax.broadcasted_iota(jnp.int32, (4, slots), 1)
+
+    def finish(d, _):
+        out_ref[d] = jnp.where(slot < live_ref[0, d], home[d, :, 0:slots], 0.0)
+        return 0
+
+    lax.fori_loop(0, n, finish, 0)
 
 
 def local(
@@ -323,27 +335,20 @@
     reactions = frequency_factor.shape[0]
     slots = particle_voxel_position.shape[2]
     padded = (reactions + 7) // 8 * 8
-    fill = lambda a, v: jnp.pad(a, (0, 256 - a.shape[0]), constant_values=v)
-    par = jnp.stack(
-        [
-            fill(frequency_factor, 1.0),
-            fill(arrhenius_barrier, 0.0),
-            fill(species_mass_unit, 1.0),
-            fill(formation_energy, 0.0),
-        ]
-    )
     vmem = pl.BlockSpec(memory_space=pltpu.VMEM)
     dma = pltpu.SemaphoreType.DMA
-    returned = pl.pallas_call(
+    samples = pl.pallas_call(
         functools.partial(kernel, n),
-        out_shape=jax.ShapeDtypeStruct((n, 4, 128), f32),
-        in_specs=[pl.BlockSpec(memory_space=pl.ANY)] + [vmem] * 6,
+        out_shape=jax.ShapeDtypeStruct((n, 4, slots), f32),
+        in_specs=[pl.BlockSpec(memory_space=pl.ANY)] + [vmem] * 9
+        + [pl.BlockSpec(memory_space=pltpu.SMEM)],
         out_specs=vmem,
         scratch_shapes=[
             pltpu.VMEM((planes, n_species, ny, nz), f32),
             pltpu.VMEM((32 * ny, nz), f32),
             pltpu.VMEM((padded, 128), bf16),
             pltpu.VMEM((padded, 128), f32),
+            pltpu.VMEM((128, (padded + 127) // 128 * 128), f32),
             pltpu.VMEM((planes * ny, nz), f32),
             pltpu.VMEM(((planes + 1) * 4 * ny, 2 * nz), bf16),
             pltpu.VMEM((reach, ny, nz), f32),
@@ -368,13 +373,16 @@
         component_shares,
         thermal_ratio,
         fuel_share,
-        par,
-        product_minus_reactant,
+        species_mass_unit[None],
+        formation_energy[None],
+        frequency_factor[None],
+        arrhenius_barrier[None],
+        product_minus_reactant.T,
         particle_voxel_position[0],
-        particle_voxel_offset[0],
+        jnp.transpose(particle_voxel_offset[0], (1, 0, 2)),
+        particle_active_total,
     )
-    live_slot = jnp.arange(slots, dtype=jnp.int32)[None, :] < particle_active_total[0][:, None]
-    return jnp.where(live_slot[:, None, :], returned[:, :, 0:slots], f32(0.0))[None]
+    return samples[None]
 
 
 def solution(mesh):

time: 29.5 us -> 22.5 us (0.76)
  local copies, waits for them, and re-layouts: 5.54 us -> 1.38 us
  other arithmetic: 2.06 us -> 0 us
  Pallas kernels: 21.5 us -> 20.8 us
    pad x4 -> x0, local copies, waits for them, and re-layouts: 2.68 us -> none  [local(): fill = lambda a, v: jnp.pad(a, (0, 256 - a.shape[0]), constant_values=v)]
    unnamed x4 -> x1, local copies, waits for them, and re-layouts: 2.86 us -> 1.38 us
    broadcast_in_dim x1 -> x0, other arithmetic: 1.39 us -> none  [local(): jnp.where(live_slot[:, None, :], returned[:, :, 0:slots], f32(0.0))[None]]
    pallas_call x1, Pallas kernels: 21.5 us -> 20.8 us  [local(): pl.pallas_call(functools.partial(kernel, n), out_shape=jax.ShapeDtypeStru...]
    another operation x1 -> x0, other arithmetic: 0.6 us -> none  [local(): jnp.stack([fill(frequency_factor, 1.0), fill(arrhenius_barrier, 0.0), fil...]
where the time goes in v2:
time: 22.5 us; the launch traced here: 22.2 us
  Pallas kernels  20.8 us (92%)
  local copies, waits for them, and re-layouts  1.38 us (6%)
    pallas_call x1, Pallas kernels, local(): pl.pallas_call(functools.partial(kernel, n), out_shape=jax.ShapeDtypeStru...  20.8 us
    unnamed x1, local copies, waits for them, and re-layouts  1.38 us

profile of v2, /device:TPU:0, one launch (start us, length us, event | category | flops | bytes accessed | tf_op | source)
XLA Modules:
  0.0 22.2 jit_solution(12472029625885153116)
XLA Ops:
  0.0 20.8 %shard_map.109 = f32[16,4,64]{2,1,0:T(4,128)} custom-call(f32[22,5,32,128]{3,2,1,0:T(8,128)} %species_hbm.1, f32[5,32,128]{2,1,0:T(8,128)} %t_ref.1, f32[5,32,128]{2,1,0:T(8,128)} %fuel_ref.1, f32[1,22]{1,0:T(1,128)} %bitcast.16, f32[1,22]{1,0:T(1,128)} %bitcast.17, f32[1,206]{1,0:T(1,128)} %bitcast.14, f32[1,206]{1,0:T(1,128)} %bitcast.15, ...), custom_call_target="tpu_custom_call" | custom-call | tf_op jit(solution)/shard_map/pallas_call | solution.py:340
  20.8 1.4 %copy.13 = f32[1,16,4,64]{3,2,1,0:T(4,128)} copy(f32[1,16,4,64]{3,2,1,0:T(4,128)} %bitcast.10) | data formatting | bytes 32768

commit v3 on v2

--- a/solution.py
+++ b/solution.py
@@ -124,11 +124,16 @@
     weights[...] = columns.astype(bf16)
     heat_weight[...] = jnp.broadcast_to(columns[:, 3 * group : 3 * group + 1], (padded, 128))
 
+    step = ny + 1
+
+    def put_feat(j, value):
+        feat[j * step : j * step + ny, :] = value
+
     ones = jnp.ones((ny, nz), f32)
     for j in range(3):
-        feat[(n_species + 3 + j) * ny : (n_species + 4 + j) * ny, :] = ones
+        put_feat(n_species + 3 + j, ones)
     for j in range(n_species + 6, group):
-        feat[j * ny : (j + 1) * ny, :] = jnp.zeros((ny, nz), f32)
+        put_feat(j, jnp.zeros((ny, nz), f32))
 
     batch = 32
 
@@ -137,18 +142,18 @@
         temper = t_ref[p]
         log_t = jnp.log(temper)
         for s in range(n_species):
-            feat[s * ny : (s + 1) * ny, :] = (jnp.log(species[p, s]) - log_t) * log2e
+            put_feat(s, (jnp.log(species[p, s]) - log_t) * log2e)
         inverse = 1.0 / temper
         for j in range(3):
-            feat[(n_species + j) * ny : (n_species + j + 1) * ny, :] = inverse
+            put_feat(n_species + j, inverse)
 
         def rows(i, _):
             for b in range(0, batch, 2):
                 r = i * batch + b
                 f = jnp.concatenate(
                     [
-                        feat[pl.ds(r, group, stride=ny), :],
-                        feat[pl.ds(r + 1, group, stride=ny), :],
+                        feat[pl.ds(r, group, stride=step), :],
+                        feat[pl.ds(r + 1, group, stride=step), :],
                     ],
                     axis=1,
                 )
@@ -256,8 +261,8 @@
     z_label = lax.broadcasted_iota(jnp.int32, (nz, 256), 0).astype(f32)
     y_label = lax.broadcasted_iota(jnp.int32, (ny, 256), 0).astype(f32)
 
-    def sample(step, _):
-        g = lax.rem(me // 4 + 1 + step, n // 4)
+    def sample(turn, _):
+        g = lax.rem(me // 4 + 1 + turn, n // 4)
         halves = [
             jnp.where(low, recv[4 * g + 2 * h], pltpu.roll(recv[4 * g + 2 * h + 1], slots, 1))
             for h in range(2)
@@ -345,7 +350,7 @@
         out_specs=vmem,
         scratch_shapes=[
             pltpu.VMEM((planes, n_species, ny, nz), f32),
-            pltpu.VMEM((32 * ny, nz), f32),
+            pltpu.VMEM((32 * (ny + 1), nz), f32),
             pltpu.VMEM((padded, 128), bf16),
             pltpu.VMEM((padded, 128), f32),
             pltpu.VMEM((128, (padded + 127) // 128 * 128), f32),

time: 22.5 us -> 22.1 us (0.982)
  Pallas kernels: 20.8 us -> 20.5 us
    pallas_call x1, Pallas kernels: 20.8 us -> 20.5 us  [local(): pl.pallas_call(functools.partial(kernel, n), out_shape=jax.ShapeDtypeStru...]
where the time goes in v3:
time: 22.1 us; the launch traced here: 21.9 us
  Pallas kernels  20.5 us (93%)
  local copies, waits for them, and re-layouts  1.38 us (6%)
    pallas_call x1, Pallas kernels, local(): pl.pallas_call(functools.partial(kernel, n), out_shape=jax.ShapeDtypeStru...  20.5 us
    unnamed x1, local copies, waits for them, and re-layouts  1.38 us

profile of v3, /device:TPU:0, one launch (start us, length us, event | category | flops | bytes accessed | tf_op | source)
XLA Modules:
  0.0 21.9 jit_solution(4131138781797001784)
XLA Ops:
  0.0 20.5 %shard_map.109 = f32[16,4,64]{2,1,0:T(4,128)} custom-call(f32[22,5,32,128]{3,2,1,0:T(8,128)} %species_hbm.1, f32[5,32,128]{2,1,0:T(8,128)} %t_ref.1, f32[5,32,128]{2,1,0:T(8,128)} %fuel_ref.1, f32[1,22]{1,0:T(1,128)} %bitcast.16, f32[1,22]{1,0:T(1,128)} %bitcast.17, f32[1,206]{1,0:T(1,128)} %bitcast.14, f32[1,206]{1,0:T(1,128)} %bitcast.15, ...), custom_call_target="tpu_custom_call" | custom-call | tf_op jit(solution)/shard_map/pallas_call | solution.py:345
  20.5 1.4 %copy.13 = f32[1,16,4,64]{3,2,1,0:T(4,128)} copy(f32[1,16,4,64]{3,2,1,0:T(4,128)} %bitcast.10) | data formatting | bytes 32768
